TPU v7x, 32 devices: a whole 2x2x4 slice. The times are simulated.
32 devices in a mesh: tp: 8 (over y, x, core), dp: 4 (over z).
Axes of the slice: x: 2, y: 2, z: 4, core: 2. Of those that a mesh axis runs over, the one named last changes fastest.
Arguments:
- activations: bfloat16 [64, 512, 4096], P('dp', None, 'tp'), may hold values from -6 to 6
- query_output_cotangent: bfloat16 [64, 512, 4096], P('dp', None, 'tp'), may hold values from -6 to 6
- value_output_cotangent: bfloat16 [64, 512, 4096], P('dp', None, 'tp'), may hold values from -6 to 6
- lengths: int32 [64], P('dp'), may hold values from 1 to 512
- reducing_matrices_pair: bfloat16 [2, 4096, 128], P(None, 'tp'), may hold values from -0.09375 to 0.09375
- expanding_matrices_pair: bfloat16 [2, 128, 4096], P(None, None, 'tp'), may hold values from -0.5 to 0.5
- width_side_projections: bfloat16 [2, 4096, 128], P(None, 'tp'), may hold values from -0.09375 to 0.09375
- narrow_random_sketch: bfloat16 [128, 16], replicated, may hold values from -0.5 to 0.5
- projected_first_moment: float32 [8192], replicated, may hold values from -6 to 6
- projected_second_moment: float32 [8192], replicated, may hold values from 0.1 to 10
- targets: bfloat16 [1024, 8192], P('dp', 'tp'), may hold values from -6 to 6
Outputs:
- scores: float32 [64, 1024], P('dp', 'tp')
All inputs are finite; a program needn't handle non-finite values.
Results may differ from a plain program's by a relative error of at most 0.023.
Values may be sent and summed in bfloat16 or wider, within the bound.
A program may use at most 128 MiB of HBM per device.

v0:
```python
import math
import jax
import jax.numpy as jnp
from jax import lax
from jax.sharding import PartitionSpec as P


def adam_update(features, first_moment, second_moment):
    mixed = 0.9 * first_moment + 0.1 * features
    spread = 0.999 * second_moment + 0.001 * features * features
    return mixed / (jnp.sqrt(spread) + 1e-08)


def combine_factors(reducing_matrices_pair, expanding_matrices_pair, narrow_random_sketch):
    attention_key_reducer = jnp.dot(
        reducing_matrices_pair[0], narrow_random_sketch, preferred_element_type=jnp.float32
    ).astype(jnp.bfloat16)
    value_down_factor = jnp.dot(
        reducing_matrices_pair[1], narrow_random_sketch, preferred_element_type=jnp.float32
    ).astype(jnp.bfloat16)
    query_up_factor = jnp.dot(
        expanding_matrices_pair[0].T, narrow_random_sketch, preferred_element_type=jnp.float32
    ).astype(jnp.bfloat16)
    value_up_factor = jnp.dot(
        expanding_matrices_pair[1].T, narrow_random_sketch, preferred_element_type=jnp.float32
    ).astype(jnp.bfloat16)
    return (attention_key_reducer, value_down_factor, query_up_factor, value_up_factor)


def body(
    activations,
    query_output_cotangent,
    value_output_cotangent,
    lengths,
    reducing_matrices_pair,
    expanding_matrices_pair,
    width_side_projections,
    narrow_random_sketch,
    projected_first_moment,
    projected_second_moment,
    targets,
):
    attention_key_reducer, value_down_factor, query_up_factor, value_up_factor = combine_factors(
        reducing_matrices_pair, expanding_matrices_pair, narrow_random_sketch
    )
    rank_cols = narrow_random_sketch.shape[1]
    w_left = jnp.concatenate(
        [attention_key_reducer, value_down_factor, width_side_projections[0]], axis=1
    )
    w_query = jnp.concatenate([query_up_factor, width_side_projections[1]], axis=1)
    w_value = jnp.concatenate([value_up_factor, width_side_projections[1]], axis=1)
    groups = lax.axis_size("tp")
    parts = lax.axis_size("dp")
    member = lax.axis_index("tp")
    local_ex, seq_len = activations.shape[:2]
    feature_count = projected_first_moment.shape[0]
    positions = jnp.arange(seq_len, dtype=jnp.int32)
    token_mask = (positions[None, :] < lengths[:, None])[..., None]

    def project(rows, weights):
        out = jnp.einsum("esd,dc->esc", rows, weights, preferred_element_type=jnp.float32)
        return out.astype(jnp.bfloat16)

    left = project(activations, w_left)
    right_q = project(query_output_cotangent, w_query)
    right_v = project(value_output_cotangent, w_value)
    narrow = jnp.concatenate(
        [left[..., : 2 * rank_cols], right_q[..., :rank_cols], right_v[..., :rank_cols]], axis=-1
    )
    narrow = jnp.where(token_mask, narrow, jnp.zeros((), jnp.bfloat16))
    narrow = lax.psum(narrow, "tp")

    def outer_sum(first, wide):
        return jnp.einsum(
            "esr,esk->erk",
            narrow[..., first * rank_cols : (first + 1) * rank_cols],
            wide,
            preferred_element_type=jnp.float32,
        )

    own_features = jnp.concatenate(
        [
            outer_sum(2, left[..., 2 * rank_cols :]),
            outer_sum(3, left[..., 2 * rank_cols :]),
            outer_sum(0, right_q[..., rank_cols:]),
            outer_sum(1, right_v[..., rank_cols:]),
        ],
        axis=1,
    ).reshape(local_ex, -1)
    features = lax.psum_scatter(
        own_features.astype(jnp.bfloat16), "tp", scatter_dimension=1, tiled=True
    ).astype(jnp.float32)
    span = feature_count // groups
    first_moment = lax.dynamic_slice_in_dim(projected_first_moment, member * span, span)
    second_moment = lax.dynamic_slice_in_dim(projected_second_moment, member * span, span)
    update = adam_update(features, first_moment, second_moment).astype(jnp.bfloat16)
    update = lax.all_gather(update, "dp", axis=0, tiled=True)
    wide_update = update.astype(jnp.float32)
    target_float = targets.astype(jnp.float32)
    update_sq = jnp.sum(wide_update * wide_update, axis=1)
    target_sq = jnp.sum(target_float * target_float, axis=1)
    dots = lax.dot_general(
        update, targets, (((1,), (1,)), ((), ())), preferred_element_type=jnp.float32
    )
    rows = jnp.concatenate(
        [dots, jnp.broadcast_to(update_sq[:, None], (dots.shape[0], 128))], axis=1
    ).reshape(parts, local_ex, -1)
    extra = jnp.pad(target_sq, (0, 128))
    rows = jnp.concatenate([rows, jnp.broadcast_to(extra, (parts, 8, extra.shape[0]))], axis=1)
    rows = lax.psum(rows, "tp")
    rows = lax.all_to_all(rows, "dp", split_axis=0, concat_axis=0, tiled=True)
    owned = targets.shape[0]
    totals = jnp.moveaxis(rows[:, :, :owned], 0, 1).reshape(local_ex + 8, parts * owned)
    columns = parts * owned // groups
    totals = lax.dynamic_slice_in_dim(totals, member * columns, columns, 1)
    row_scale = lax.rsqrt(rows[0, :local_ex, owned : owned + 1] + 1e-06)
    column_scale = lax.rsqrt(totals[local_ex : local_ex + 1] + 1e-06)
    return totals[:local_ex] * row_scale * column_scale * math.sqrt(feature_count)


def solution(mesh):
    placed = (
        P("dp", None, "tp"),
        P("dp", None, "tp"),
        P("dp", None, "tp"),
        P("dp"),
        P(None, "tp", None),
        P(None, None, "tp"),
        P(None, "tp", None),
        P(),
        P(),
        P(),
        P("dp", "tp"),
    )
    return jax.shard_map(body, mesh=mesh, in_specs=placed, out_specs=P("dp", "tp"), check_vma=False)
```

profile of v0, /device:TPU:0, one launch (start us, length us, event | category | flops | bytes accessed | tf_op | source)
XLA Modules:
  0.0 220.2 jit_solution(16352123582546980845)
XLA Ops:
  6.5 0.0 copy-start
  6.5 0.0 all-reduce.4.cloned.1.call-start
  6.5 0.7 copy-done
  7.2 1.0 convolution_convert_fusion.2
  8.3 1.1 convolution_convert_fusion.3
  9.3 1.0 convolution_convert_fusion.1
  10.4 1.0 convolution_convert_fusion
  11.4 1.0 fusion.55
  12.4 0.1 copy.37
  12.5 6.3 %convert_bitcast_fusion = bf16[16,512,160]{1,2,0:T(8,128)(2,1)S(1)} fusion(bf16[16,512,512]{2,1,0:T(8,128)(2,1)} %param.11, bf16[512,128]{0,1:T(8,128)(2,1)S(1)} %bitcast.53, bf16[512,16]{0,1:T(8,128)(2,1)S(1)} %convolution_convert_fusion.2, bf16[512,16]{0,1:T(8,128)(2,1)S(1)} %convolution_convert_fusion.3), kind=kOutput, calls=%fused_computation | convolution fusion | flops 1343979520 | bytes 11173888 | tf_op jit(solution)/shard_map/esd,dc->esc/dot_general | solution.py:61
  18.8 0.0 copy-start.1
  18.8 0.1 copy.38
  18.9 7.1 %convert_bitcast_fusion.2 = bf16[16,512,144]{1,2,0:T(8,128)(2,1)S(1)} fusion(bf16[16,512,512]{2,1,0:T(8,128)(2,1)} %param.12, bf16[512,16]{0,1:T(8,128)(2,1)S(1)} %convolution_convert_fusion.1, bf16[512,128]{0,1:T(8,128)(2,1)S(1)} %bitcast.49), kind=kOutput, calls=%fused_computation.2 | convolution fusion | flops 1209434112 | bytes 10895360 | tf_op jit(solution)/shard_map/esd,dc->esc/dot_general | solution.py:61
  26.0 0.0 copy-done.1
  26.0 0.0 copy-start.3
  26.1 0.0 copy-start.8
  26.1 0.0 slice-start
  26.1 7.1 %convert_bitcast_fusion.1 = bf16[16,512,144]{1,2,0:T(8,128)(2,1)S(1)} fusion(bf16[16,512,512]{2,1,0:T(8,128)(2,1)} %param.13, bf16[512,16]{0,1:T(8,128)(2,1)S(1)} %convolution_convert_fusion, bf16[512,128]{0,1:T(8,128)(2,1)S(1)} %bitcast.50), kind=kOutput, calls=%fused_computation.1 | convolution fusion | flops 1209434112 | bytes 10895360 | tf_op jit(solution)/shard_map/esd,dc->esc/dot_general | solution.py:61
  33.2 0.0 copy-done.3
  33.2 0.0 copy-start.5
  33.2 0.0 copy-start.2
  33.2 1.4 copy-done.5
  34.6 0.0 copy-done.8
  34.6 0.1 iota_compare_fusion
  34.7 0.0 slice-done
  34.7 1.3 maximum_select_fusion
  36.0 0.0 all-reduce.4.cloned.1.call-update
  36.0 0.0 reduce-scatter.2.cloned.1.call-start
  36.1 59.4 %all-reduce.4.cloned.1.call-done = bf16[16,512,64]{1,2,0:T(8,128)(2,1)} async-done(((bf16[16,512,64]{1,2,0:T(8,128)(2,1)}), bf16[16,512,64]{1,2,0:T(8,128)(2,1)}) %all-reduce.4.cloned.1.call-update) | async-done | bytes 1048592 | tf_op jit(solution)/shard_map/psum | solution.py:71
  95.5 0.0 copy-done.2
  95.5 0.0 copy-start.4
  95.5 0.0 copy-start.9
  95.5 1.7 fusion.8
  97.2 0.0 copy-start.6
  97.2 1.8 fusion.11
  99.0 0.0 copy-done.4
  99.0 0.0 copy-done.9
  99.0 0.0 copy-start.7
  99.0 0.6 fusion.14
  99.7 0.0 copy-done.6
  99.7 0.7 fusion.17
  100.4 0.9 copy.42
  101.2 0.0 reduce-scatter.2.cloned.1.call-update
  101.3 0.0 all-reduce.6.cloned.1.call-start
  101.3 0.0 copy-done.7
  101.3 0.2 multiply_reduce_fusion
  101.5 0.7 dynamic-slice_multiply_fusion.1
  102.2 31.9 %reduce-scatter.2.cloned.1.call-done = bf16[16,1024]{1,0:T(8,128)(2,1)} async-done(((bf16[16,8192]{1,0:T(8,128)(2,1)}), bf16[16,1024]{1,0:T(8,128)(2,1)}) %reduce-scatter.2.cloned.1.call-update) | async-done | bytes 32784 | tf_op jit(solution)/shard_map/reduce_scatter | solution.py:90
  134.1 0.8 fusion.42
  134.9 13.5 %all_gather.3 = bf16[64,1024]{1,0:T(8,128)(2,1)S(1)} all-gather(bf16[16,1024]{1,0:T(8,128)(2,1)S(1)} %fusion.42), channel_id=1, replica_groups=mesh['tp'=8,'dp'=4] {'dp'}, dimensions={0}, use_global_device_ids=true | all-gather | bytes 163840 | tf_op jit(solution)/shard_map/all_gather | solution.py:97
  148.4 0.3 fusion.56
  148.7 0.1 multiply_reduce_fusion.1
  148.8 0.1 broadcast_in_dim.28
  148.9 0.7 pad_maximum_fusion.1
  149.6 0.0 all-reduce.6.cloned.1.call-update
  149.6 52.0 %all-reduce.6.cloned.1.call-done = f32[4,24,384]{2,1,0:T(8,128)} async-done(((f32[4,24,384]{2,1,0:T(8,128)}), f32[4,24,384]{2,1,0:T(8,128)}) %all-reduce.6.cloned.1.call-update) | async-done | bytes 147472 | tf_op jit(solution)/shard_map/psum | solution.py:110
  201.6 4.6 %all-to-all-start = ((f32[4,24,384]{2,1,0:T(8,128)}), f32[4,24,384]{2,1,0:T(8,128)S(1)}, u32[]{:S(2)}, u32[]{:S(2)}) async-start(f32[4,24,384]{2,1,0:T(8,128)} %all-reduce.6.cloned.1.call-done), calls=%async_computation.1 | async-start | bytes 294912 | tf_op jit(solution)/shard_map/all_to_all | solution.py:111
  206.2 6.6 %all-to-all-done = f32[4,24,384]{2,1,0:T(8,128)S(1)} async-done(((f32[4,24,384]{2,1,0:T(8,128)}), f32[4,24,384]{2,1,0:T(8,128)S(1)}, u32[]{:S(2)}, u32[]{:S(2)}) %all-to-all-start) | async-done | bytes 147488 | tf_op jit(solution)/shard_map/all_to_all | solution.py:111
  212.9 0.1 fusion.47
  213.0 0.7 fusion.49
  (9 shorter events, 0.1 us)
Async XLA Ops:
  6.5 0.7 copy-start
  6.5 88.9 %all-reduce.4.cloned.1.call-start = ((), (), s32[]{:S(2)}) async-start(), calls=%async_computation.2 | async-start | bytes 2097152 | tf_op jit(solution)/shard_map/psum | solution.py:71
  18.8 7.2 %copy-start.1 = (bf16[16,512,160]{1,2,0:T(8,128)(2,1)}, bf16[16,512,160]{1,2,0:T(8,128)(2,1)S(1)}, u32[]{:S(2)}) copy-start(bf16[16,512,160]{1,2,0:T(8,128)(2,1)S(1)} %convert_bitcast_fusion) | copy-start | bytes 7864324
  26.0 7.2 %copy-start.3 = (bf16[16,512,144]{1,2,0:T(8,128)(2,1)}, bf16[16,512,144]{1,2,0:T(8,128)(2,1)S(1)}, u32[]{:S(2)}) copy-start(bf16[16,512,144]{1,2,0:T(8,128)(2,1)S(1)} %convert_bitcast_fusion.2) | copy-start | bytes 7077892
  26.1 8.6 %copy-start.8 = (s32[16]{0:T(128)S(1)}, s32[16]{0:T(128)}, u32[]{:S(2)}) copy-start(s32[16]{0:T(128)} %param.14) | copy-start | bytes 196
  26.1 8.6 %slice-start = ((bf16[16,512,160]{1,2,0:T(8,128)(2,1)}), bf16[16,512,32]{1,2,0:T(8,128)(2,1)S(1)}, s32[]{:S(2)}) async-start(bf16[16,512,160]{1,2,0:T(8,128)(2,1)} %copy-done.1), calls=%async_computation.5 | async-start | bytes 1048576 | tf_op jit(solution)/shard_map/slice | solution.py:68
  33.2 1.4 copy-start.5
  33.2 62.3 %copy-start.2 = (bf16[16,512,160]{1,2,0:T(8,128)(2,1)S(1)}, bf16[16,512,160]{1,2,0:T(8,128)(2,1)}, u32[]{:S(2)}) copy-start(bf16[16,512,160]{1,2,0:T(8,128)(2,1)} %copy-done.1) | copy-start | bytes 7864324
  36.0 98.1 %reduce-scatter.2.cloned.1.call-start = ((), (), s32[]{:S(2)}) async-start(), calls=%async_computation.3 | async-start | bytes 294912 | tf_op jit(solution)/shard_map/reduce_scatter | solution.py:90
  95.5 3.5 %copy-start.4 = (bf16[16,512,144]{1,2,0:T(8,128)(2,1)S(1)}, bf16[16,512,144]{1,2,0:T(8,128)(2,1)}, u32[]{:S(2)}) copy-start(bf16[16,512,144]{1,2,0:T(8,128)(2,1)} %copy-done.3) | copy-start | bytes 7077892
  95.5 3.5 %copy-start.9 = (bf16[16,512,64]{1,2,0:T(8,128)(2,1)S(1)}, bf16[16,512,64]{1,2,0:T(8,128)(2,1)}, u32[]{:S(2)}) copy-start(bf16[16,512,64]{1,2,0:T(8,128)(2,1)} %all-reduce.4.cloned.1.call-done) | copy-start | bytes 3145732
  97.2 2.4 %copy-start.6 = (bf16[16,512,144]{1,2,0:T(8,128)(2,1)S(1)}, bf16[16,512,144]{1,2,0:T(8,128)(2,1)}, u32[]{:S(2)}) copy-start(bf16[16,512,144]{1,2,0:T(8,128)(2,1)} %copy-done.5) | copy-start | bytes 7077892
  99.0 2.3 %copy-start.7 = (bf16[256,1024]{1,0:T(8,128)(2,1)S(1)}, bf16[256,1024]{1,0:T(8,128)(2,1)}, u32[]{:S(2)}) copy-start(bf16[256,1024]{1,0:T(8,128)(2,1)} %param.21) | copy-start | bytes 1572868
  101.3 100.4 %all-reduce.6.cloned.1.call-start = ((), (), s32[]{:S(2)}) async-start(), calls=%async_computation.4 | async-start | bytes 294912 | tf_op jit(solution)/shard_map/psum | solution.py:110
  201.6 11.2 %all-to-all-start = ((f32[4,24,384]{2,1,0:T(8,128)}), f32[4,24,384]{2,1,0:T(8,128)S(1)}, u32[]{:S(2)}, u32[]{:S(2)}) async-start(f32[4,24,384]{2,1,0:T(8,128)} %all-reduce.6.cloned.1.call-done), calls=%async_computation.1 | async-start | bytes 294912 | tf_op jit(solution)/shard_map/all_to_all | solution.py:111
Sparse Core Ops, SparseCore 0:
  36.1 59.2 all-reduce.3
  101.4 32.6 reduce-scatter.1
  149.8 51.8 all-reduce.5
where the time goes:
time: 221 us; the launch traced here: 220 us
  waiting for transfers between devices  150 us (68%)
  matrix products  29.7 us (13%)
  blocking collectives  13.5 us (6%)
  between operations  13.3 us (6%)
  other arithmetic  4.71 us (2%)
  starting transfers between devices  4.69 us (2%)
  local copies, waits for them, and re-layouts  4.36 us (2%)
    psum x1, waiting for transfers between devices, body(): narrow = lax.psum(narrow, 'tp')  59.4 us
    psum x1, waiting for transfers between devices, body(): rows = lax.psum(rows, 'tp')  52 us
    reduce_scatter x1, waiting for transfers between devices, body(): lax.psum_scatter(own_features.astype(jnp.bfloat16), 'tp', scatter_dimensi...  31.9 us
    dot_general x3, matrix products, project(): jnp.einsum('esd,dc->esc', rows, weights, preferred_element_type=jnp.float32)  20.4 us
    all_gather x1, blocking collectives, body(): update = lax.all_gather(update, 'dp', axis=0, tiled=True)  13.5 us
    all_to_all x1, waiting for transfers between devices, body(): rows = lax.all_to_all(rows, 'dp', split_axis=0, concat_axis=0, tiled=True)  6.65 us
    dot_general x4, matrix products, outer_sum(): jnp.einsum('esr,esk->erk', narrow[..., first * rank_cols:(first + 1) * ra...  4.82 us
    all_to_all x1, starting transfers between devices, body(): rows = lax.all_to_all(rows, 'dp', split_axis=0, concat_axis=0, tiled=True)  4.6 us
  transfers between devices with their start and end apart: 4, of which 4 were waited for; matrix products, arithmetic and copies ran while one was open for 0% of the time, Pallas kernels for 0%

commit v1 on v0

--- a/solution.py
+++ b/solution.py
@@ -3,6 +3,24 @@
 import jax.numpy as jnp
 from jax import lax
 from jax.sharding import PartitionSpec as P
+
+
+def collect(shard, axis, dim):
+    ways, here, step = (lax.axis_size(axis), lax.axis_index(axis), shard.shape[dim])
+    lengths = [n * ways if d == dim else n for d, n in enumerate(shard.shape)]
+    full = lax.dynamic_update_slice_in_dim(
+        jnp.zeros(lengths, shard.dtype), shard, here * step, axis=dim
+    )
+    going_up = going_down = shard
+    for far in range(1, ways // 2 + 1):
+        going_up = lax.ppermute(going_up, axis, [(d, (d + 1) % ways) for d in range(ways)])
+        full = lax.dynamic_update_slice_in_dim(full, going_up, (here - far) % ways * step, axis=dim)
+        if 2 * far < ways:
+            going_down = lax.ppermute(going_down, axis, [(d, (d - 1) % ways) for d in range(ways)])
+            full = lax.dynamic_update_slice_in_dim(
+                full, going_down, (here + far) % ways * step, axis=dim
+            )
+    return full
 
 
 def adam_update(features, first_moment, second_moment):
@@ -94,7 +112,7 @@
     first_moment = lax.dynamic_slice_in_dim(projected_first_moment, member * span, span)
     second_moment = lax.dynamic_slice_in_dim(projected_second_moment, member * span, span)
     update = adam_update(features, first_moment, second_moment).astype(jnp.bfloat16)
-    update = lax.all_gather(update, "dp", axis=0, tiled=True)
+    update = collect(update, "dp", 0)
     wide_update = update.astype(jnp.float32)
     target_float = targets.astype(jnp.float32)
     update_sq = jnp.sum(wide_update * wide_update, axis=1)

time: 221 us -> 216 us (0.977)
  blocking collectives: 13.5 us -> 0 us
  waiting for transfers between devices: 150 us -> 155 us
  starting transfers between devices: 4.69 us -> 8.62 us
    all_gather x1 -> x0, blocking collectives: 13.5 us -> none  [body(): update = lax.all_gather(update, 'dp', axis=0, tiled=True)]
    ppermute x0 -> x3, waiting for transfers between devices: none -> 7.6 us  [the longest x2 7.59 us: collect(): lax.ppermute(going_up, axis, [(d, (d + 1) % ways) for d in range(ways)])]
    ppermute x0 -> x3, starting transfers between devices: none -> 3.93 us  [the longest x1 2.4 us: collect(): lax.ppermute(going_down, axis, [(d, (d - 1) % ways) for d in range(ways)])]
    psum x1, waiting for transfers between devices: 52 us -> 49.3 us  [body(): rows = lax.psum(rows, 'tp')]
  transfers between devices with their start and end apart: 4 -> 7, of which waited for: 4 -> 6; matrix products, arithmetic and copies ran while one was open for 0% -> 0% of each run, Pallas kernels for 0% -> 0%
where the time goes in v1:
time: 216 us
  waiting for transfers between devices  155 us (72%)
  matrix products  29.7 us (14%)
  between operations  13.4 us (6%)
  starting transfers between devices  8.62 us (4%)
  other arithmetic  4.73 us (2%)
  local copies, waits for them, and re-layouts  4.39 us (2%)
    psum x1, waiting for transfers between devices, body(): narrow = lax.psum(narrow, 'tp')  59.4 us
    psum x1, waiting for transfers between devices, body(): rows = lax.psum(rows, 'tp')  49.3 us
    reduce_scatter x1, waiting for transfers between devices, body(): lax.psum_scatter(own_features.astype(jnp.bfloat16), 'tp', scatter_dimensi...  32.1 us
    dot_general x3, matrix products, project(): jnp.einsum('esd,dc->esc', rows, weights, preferred_element_type=jnp.float32)  20.4 us
    ppermute x2, waiting for transfers between devices, collect(): lax.ppermute(going_up, axis, [(d, (d + 1) % ways) for d in range(ways)])  7.59 us
    all_to_all x1, waiting for transfers between devices, body(): rows = lax.all_to_all(rows, 'dp', split_axis=0, concat_axis=0, tiled=True)  6.65 us
    dot_general x4, matrix products, outer_sum(): jnp.einsum('esr,esk->erk', narrow[..., first * rank_cols:(first + 1) * ra...  4.83 us
    all_to_all x1, starting transfers between devices, body(): rows = lax.all_to_all(rows, 'dp', split_axis=0, concat_axis=0, tiled=True)  4.6 us
  transfers between devices with their start and end apart: 7, of which 6 were waited for; matrix products, arithmetic and copies ran while one was open for 0% of the time, Pallas kernels for 0%

profile of v1, /device:TPU:0, one launch (start us, length us, event | category | flops | bytes accessed | tf_op | source)
XLA Modules:
  0.0 215.9 jit_solution(307987081440048355)
XLA Ops:
  6.5 0.0 copy-start
  6.5 0.0 all-reduce.4.cloned.1.call-start
  6.5 0.7 copy-done
  7.2 1.0 convolution_convert_fusion.2
  8.3 1.1 convolution_convert_fusion.3
  9.3 1.0 convolution_convert_fusion.1
  10.4 1.0 convolution_convert_fusion
  11.4 1.0 fusion.56
  12.4 0.1 copy.37
  12.5 6.3 %convert_bitcast_fusion = bf16[16,512,160]{1,2,0:T(8,128)(2,1)S(1)} fusion(bf16[16,512,512]{2,1,0:T(8,128)(2,1)} %param.11, bf16[512,128]{0,1:T(8,128)(2,1)S(1)} %bitcast.53, bf16[512,16]{0,1:T(8,128)(2,1)S(1)} %convolution_convert_fusion.2, bf16[512,16]{0,1:T(8,128)(2,1)S(1)} %convolution_convert_fusion.3), kind=kOutput, calls=%fused_computation | convolution fusion | flops 1343979520 | bytes 11173888 | tf_op jit(solution)/shard_map/esd,dc->esc/dot_general | solution.py:79
  18.8 0.0 copy-start.1
  18.8 0.1 copy.38
  18.9 7.1 %convert_bitcast_fusion.2 = bf16[16,512,144]{1,2,0:T(8,128)(2,1)S(1)} fusion(bf16[16,512,512]{2,1,0:T(8,128)(2,1)} %param.12, bf16[512,16]{0,1:T(8,128)(2,1)S(1)} %convolution_convert_fusion.1, bf16[512,128]{0,1:T(8,128)(2,1)S(1)} %bitcast.49), kind=kOutput, calls=%fused_computation.2 | convolution fusion | flops 1209434112 | bytes 10895360 | tf_op jit(solution)/shard_map/esd,dc->esc/dot_general | solution.py:79
  26.0 0.0 copy-done.1
  26.0 0.0 copy-start.3
  26.1 0.0 copy-start.8
  26.1 0.0 slice-start
  26.1 7.1 %convert_bitcast_fusion.1 = bf16[16,512,144]{1,2,0:T(8,128)(2,1)S(1)} fusion(bf16[16,512,512]{2,1,0:T(8,128)(2,1)} %param.13, bf16[512,16]{0,1:T(8,128)(2,1)S(1)} %convolution_convert_fusion, bf16[512,128]{0,1:T(8,128)(2,1)S(1)} %bitcast.50), kind=kOutput, calls=%fused_computation.1 | convolution fusion | flops 1209434112 | bytes 10895360 | tf_op jit(solution)/shard_map/esd,dc->esc/dot_general | solution.py:79
  33.2 0.0 copy-done.3
  33.2 0.0 copy-start.5
  33.2 0.0 copy-start.2
  33.2 1.4 copy-done.5
  34.6 0.0 copy-done.8
  34.6 0.1 iota_compare_fusion
  34.7 0.0 slice-done
  34.7 1.3 maximum_select_fusion
  36.0 0.0 all-reduce.4.cloned.1.call-update
  36.0 0.0 reduce-scatter.2.cloned.1.call-start
  36.1 59.4 %all-reduce.4.cloned.1.call-done = bf16[16,512,64]{1,2,0:T(8,128)(2,1)} async-done(((bf16[16,512,64]{1,2,0:T(8,128)(2,1)}), bf16[16,512,64]{1,2,0:T(8,128)(2,1)}) %all-reduce.4.cloned.1.call-update) | async-done | bytes 1048592 | tf_op jit(solution)/shard_map/psum | solution.py:89
  95.5 0.0 copy-done.2
  95.5 0.0 copy-start.4
  95.5 0.0 copy-start.9
  95.5 1.7 fusion.8
  97.2 0.0 copy-start.6
  97.2 1.8 fusion.11
  99.0 0.0 copy-done.4
  99.0 0.0 copy-done.9
  99.0 0.7 fusion.14
  99.7 0.0 copy-done.6
  99.7 0.7 fusion.17
  100.4 0.9 copy.42
  101.3 0.0 reduce-scatter.2.cloned.1.call-update
  101.3 0.0 all-reduce.6.cloned.1.call-start
  101.3 0.7 dynamic-slice_multiply_fusion.1
  102.1 32.1 %reduce-scatter.2.cloned.1.call-done = bf16[16,1024]{1,0:T(8,128)(2,1)} async-done(((bf16[16,8192]{1,0:T(8,128)(2,1)}), bf16[16,1024]{1,0:T(8,128)(2,1)}) %reduce-scatter.2.cloned.1.call-update) | async-done | bytes 32784 | tf_op jit(solution)/shard_map/reduce_scatter | solution.py:108
  134.2 0.8 constant_dynamic-update-slice_fusion.3
  135.0 1.5 collective-permute-start
  136.5 0.0 copy-done.7
  136.5 0.2 multiply_reduce_fusion
  136.8 2.4 %collective-permute-start.1 = (bf16[16,1024]{1,0:T(8,128)(2,1)S(1)}, bf16[16,1024]{1,0:T(8,128)(2,1)S(1)}, u32[]{:S(2)}, u32[]{:S(2)}) collective-permute-start(bf16[16,1024]{1,0:T(8,128)(2,1)S(1)} %get-tuple-element.6), channel_id=1, source_target_pairs={{0,3},{1,0},{2,1},{3,2},{4,7},{5,4},{6,5},{7,6},{8,11},{9,8},{10,9... | collective-permute-start | bytes 98312 | tf_op jit(solution)/shard_map/ppermute | solution.py:19
  139.1 1.9 collective-permute-done
  141.1 0.0 collective-permute-start.2
  141.1 0.0 collective-permute-done.1
  141.1 5.7 %collective-permute-done.2 = bf16[16,1024]{1,0:T(8,128)(2,1)S(1)} collective-permute-done((bf16[16,1024]{1,0:T(8,128)(2,1)S(1)}, bf16[16,1024]{1,0:T(8,128)(2,1)S(1)}, u32[]{:S(2)}, u32[]{:S(2)}) %collective-permute-start.2) | collective-permute-done | bytes 32800 | tf_op jit(solution)/shard_map/ppermute | solution.py:16
  146.8 0.3 fusion.57
  147.1 0.1 multiply_reduce_fusion.1
  147.2 0.1 broadcast_in_dim.32
  147.3 0.7 pad_maximum_fusion.1
  148.0 0.0 all-reduce.6.cloned.1.call-update
  148.0 49.3 %all-reduce.6.cloned.1.call-done = f32[4,24,384]{2,1,0:T(8,128)} async-done(((f32[4,24,384]{2,1,0:T(8,128)}), f32[4,24,384]{2,1,0:T(8,128)}) %all-reduce.6.cloned.1.call-update) | async-done | bytes 147472 | tf_op jit(solution)/shard_map/psum | solution.py:128
  197.3 4.6 %all-to-all-start = ((f32[4,24,384]{2,1,0:T(8,128)}), f32[4,24,384]{2,1,0:T(8,128)S(1)}, u32[]{:S(2)}, u32[]{:S(2)}) async-start(f32[4,24,384]{2,1,0:T(8,128)} %all-reduce.6.cloned.1.call-done), calls=%async_computation.1 | async-start | bytes 294912 | tf_op jit(solution)/shard_map/all_to_all | solution.py:129
  201.9 6.6 %all-to-all-done = f32[4,24,384]{2,1,0:T(8,128)S(1)} async-done(((f32[4,24,384]{2,1,0:T(8,128)}), f32[4,24,384]{2,1,0:T(8,128)S(1)}, u32[]{:S(2)}, u32[]{:S(2)}) %all-to-all-start) | async-done | bytes 147488 | tf_op jit(solution)/shard_map/all_to_all | solution.py:129
  208.6 0.1 fusion.47
  208.7 0.7 fusion.49
  (14 shorter events, 0.2 us)
Async XLA Ops:
  6.5 0.7 copy-start
  6.5 88.9 %all-reduce.4.cloned.1.call-start = ((), (), s32[]{:S(2)}) async-start(), calls=%async_computation.2 | async-start | bytes 2097152 | tf_op jit(solution)/shard_map/psum | solution.py:89
  18.8 7.2 %copy-start.1 = (bf16[16,512,160]{1,2,0:T(8,128)(2,1)}, bf16[16,512,160]{1,2,0:T(8,128)(2,1)S(1)}, u32[]{:S(2)}) copy-start(bf16[16,512,160]{1,2,0:T(8,128)(2,1)S(1)} %convert_bitcast_fusion) | copy-start | bytes 7864324
  26.0 7.2 %copy-start.3 = (bf16[16,512,144]{1,2,0:T(8,128)(2,1)}, bf16[16,512,144]{1,2,0:T(8,128)(2,1)S(1)}, u32[]{:S(2)}) copy-start(bf16[16,512,144]{1,2,0:T(8,128)(2,1)S(1)} %convert_bitcast_fusion.2) | copy-start | bytes 7077892
  26.1 8.6 %copy-start.8 = (s32[16]{0:T(128)S(1)}, s32[16]{0:T(128)}, u32[]{:S(2)}) copy-start(s32[16]{0:T(128)} %param.14) | copy-start | bytes 196
  26.1 8.6 %slice-start = ((bf16[16,512,160]{1,2,0:T(8,128)(2,1)}), bf16[16,512,32]{1,2,0:T(8,128)(2,1)S(1)}, s32[]{:S(2)}) async-start(bf16[16,512,160]{1,2,0:T(8,128)(2,1)} %copy-done.1), calls=%async_computation.5 | async-start | bytes 1048576 | tf_op jit(solution)/shard_map/slice | solution.py:86
  33.2 1.4 copy-start.5
  33.2 62.3 %copy-start.2 = (bf16[16,512,160]{1,2,0:T(8,128)(2,1)S(1)}, bf16[16,512,160]{1,2,0:T(8,128)(2,1)}, u32[]{:S(2)}) copy-start(bf16[16,512,160]{1,2,0:T(8,128)(2,1)} %copy-done.1) | copy-start | bytes 7864324
  36.0 98.1 %reduce-scatter.2.cloned.1.call-start = ((), (), s32[]{:S(2)}) async-start(), calls=%async_computation.3 | async-start | bytes 294912 | tf_op jit(solution)/shard_map/reduce_scatter | solution.py:108
  95.5 3.5 %copy-start.4 = (bf16[16,512,144]{1,2,0:T(8,128)(2,1)S(1)}, bf16[16,512,144]{1,2,0:T(8,128)(2,1)}, u32[]{:S(2)}) copy-start(bf16[16,512,144]{1,2,0:T(8,128)(2,1)} %copy-done.3) | copy-start | bytes 7077892
  95.5 3.5 %copy-start.9 = (bf16[16,512,64]{1,2,0:T(8,128)(2,1)S(1)}, bf16[16,512,64]{1,2,0:T(8,128)(2,1)}, u32[]{:S(2)}) copy-start(bf16[16,512,64]{1,2,0:T(8,128)(2,1)} %all-reduce.4.cloned.1.call-done) | copy-start | bytes 3145732
  97.2 2.4 %copy-start.6 = (bf16[16,512,144]{1,2,0:T(8,128)(2,1)S(1)}, bf16[16,512,144]{1,2,0:T(8,128)(2,1)}, u32[]{:S(2)}) copy-start(bf16[16,512,144]{1,2,0:T(8,128)(2,1)} %copy-done.5) | copy-start | bytes 7077892
  99.7 36.8 %copy-start.7 = (bf16[256,1024]{1,0:T(8,128)(2,1)S(1)}, bf16[256,1024]{1,0:T(8,128)(2,1)}, u32[]{:S(2)}) copy-start(bf16[256,1024]{1,0:T(8,128)(2,1)} %param.21) | copy-start | bytes 1572868
  101.3 96.0 %all-reduce.6.cloned.1.call-start = ((), (), s32[]{:S(2)}) async-start(), calls=%async_computation.4 | async-start | bytes 294912 | tf_op jit(solution)/shard_map/psum | solution.py:128
  135.0 6.1 %collective-permute-start = (bf16[16,1024]{1,0:T(8,128)(2,1)S(1)}, bf16[16,1024]{1,0:T(8,128)(2,1)S(1)}, u32[]{:S(2)}, u32[]{:S(2)}) collective-permute-start(bf16[16,1024]{1,0:T(8,128)(2,1)S(1)} %get-tuple-element.6), channel_id=1, source_target_pairs={{0,1},{1,2},{2,3},{3,0},{4,5},{5,6},{6,7},{7,4},{8,9},{9,10},{10,1... | collective-permute-start | bytes 98312 | tf_op jit(solution)/shard_map/ppermute | solution.py:16
  136.8 4.3 %collective-permute-start.1 = (bf16[16,1024]{1,0:T(8,128)(2,1)S(1)}, bf16[16,1024]{1,0:T(8,128)(2,1)S(1)}, u32[]{:S(2)}, u32[]{:S(2)}) collective-permute-start(bf16[16,1024]{1,0:T(8,128)(2,1)S(1)} %get-tuple-element.6), channel_id=1, source_target_pairs={{0,3},{1,0},{2,1},{3,2},{4,7},{5,4},{6,5},{7,6},{8,11},{9,8},{10,9... | collective-permute-start | bytes 98312 | tf_op jit(solution)/shard_map/ppermute | solution.py:19
  141.1 5.7 %collective-permute-start.2 = (bf16[16,1024]{1,0:T(8,128)(2,1)S(1)}, bf16[16,1024]{1,0:T(8,128)(2,1)S(1)}, u32[]{:S(2)}, u32[]{:S(2)}) collective-permute-start(bf16[16,1024]{1,0:T(8,128)(2,1)S(1)} %collective-permute-done), channel_id=1, source_target_pairs={{0,1},{1,2},{2,3},{3,0},{4,5},{5,6},{6,7},{7,4},{8,9},{9,10},{10,1... | collective-permute-start | bytes 98312 | tf_op jit(solution)/shard_map/ppermute | solution.py:16
  197.3 11.2 %all-to-all-start = ((f32[4,24,384]{2,1,0:T(8,128)}), f32[4,24,384]{2,1,0:T(8,128)S(1)}, u32[]{:S(2)}, u32[]{:S(2)}) async-start(f32[4,24,384]{2,1,0:T(8,128)} %all-reduce.6.cloned.1.call-done), calls=%async_computation.1 | async-start | bytes 294912 | tf_op jit(solution)/shard_map/all_to_all | solution.py:129
Sparse Core Ops, SparseCore 0:
  36.2 59.2 all-reduce.3
  101.4 32.6 reduce-scatter.1
  148.1 49.1 all-reduce.5
